TPU v7x, 128 devices: a whole 4x4x4 slice. The times are simulated.
128 devices in a mesh: dp: 16 (over z, y_hi, core), seq: 8 (over y_lo, x).
Axes of the slice: x: 4, y: 4 (y_hi: 2, y_lo: 2; y = y_hi * 2 + y_lo), z: 4, core: 2. Of those that a mesh axis runs over, the one named last changes fastest.
Arguments:
- tokens: bfloat16 [4096, 4096], P(('dp', 'seq')), may hold values from -6 to 6
- modality: int32 [4096], P(('dp', 'seq')), may hold values from 0 to 1, as said below
- gate_weight: bfloat16 [4096, 14336], P(None, 'dp'), may hold values from -0.09375 to 0.09375
- up_weight: bfloat16 [4096, 14336], P(None, 'dp'), may hold values from -0.09375 to 0.09375
- down_weight: bfloat16 [14336, 4096], P('dp'), may hold values from -0.046875 to 0.046875
- out_grad: bfloat16 [3072, 4096], P(('dp', 'seq')), may hold values from -1.5 to 1.5
Outputs:
- output: bfloat16 [3072, 4096], P(('dp', 'seq'))
- in_grad: bfloat16 [3072, 4096], P(('dp', 'seq'))
- gate_grad: bfloat16 [4096, 14336], P('seq', 'dp')
- up_grad: bfloat16 [4096, 14336], P('seq', 'dp')
- down_grad: bfloat16 [14336, 4096], P('dp', 'seq')
Inputs may be any that keep to these rules, and one draw needn't show every extreme that they name: In each aligned block of 32 tokens (the tokens of one device) exactly 24 tokens have modality 1 (vision); all others have 0 (text).
All inputs are finite; a program needn't handle non-finite values.
Results may differ from a plain program's by a relative error of at most 0.014.
Values may be sent and summed in bfloat16 or wider, within the bound.
A program may use at most 128 MiB of HBM per device.

v0:
```python
import jax
import jax.numpy as jnp
from jax import lax
from jax.sharding import PartitionSpec as P


def silu_parts(gate_proj):
    sigmoid_value = jax.nn.sigmoid(gate_proj)
    return (gate_proj * sigmoid_value, sigmoid_value * (1.0 + gate_proj * (1.0 - sigmoid_value)))


def contract_rows(left_matrix, right_matrix):
    return lax.dot_general(
        left_matrix, right_matrix, (((0,), (0,)), ((), ())), preferred_element_type=jnp.float32
    )


def contract_cols(left_matrix, right_matrix):
    return lax.dot_general(
        left_matrix, right_matrix, (((1,), (1,)), ((), ())), preferred_element_type=jnp.float32
    )


def on_device(tokens, modality, gate_weight, up_weight, down_weight, out_grad):
    vision_count = out_grad.shape[0]
    flags = (modality == 1).astype(jnp.int32)
    ranks = jnp.cumsum(flags) - 1
    slot_ids = jnp.arange(vision_count, dtype=jnp.int32)[:, None]
    selector = ((ranks[None, :] == slot_ids) & (flags[None, :] == 1)).astype(jnp.bfloat16)
    picked = jnp.dot(selector, tokens, preferred_element_type=jnp.float32).astype(jnp.bfloat16)
    token_rows = lax.all_gather(picked, "dp", axis=0, tiled=True)
    gate_proj = jnp.dot(token_rows, gate_weight, preferred_element_type=jnp.float32)
    up_proj = jnp.dot(token_rows, up_weight, preferred_element_type=jnp.float32)
    active, slope = silu_parts(gate_proj)
    hidden = (active * up_proj).astype(jnp.bfloat16)
    output = lax.psum_scatter(
        jnp.dot(hidden, down_weight, preferred_element_type=jnp.float32).astype(jnp.bfloat16),
        "dp",
        scatter_dimension=0,
        tiled=True,
    )
    cotangent_rows = lax.all_gather(out_grad, "dp", axis=0, tiled=True)
    back_hidden = contract_cols(cotangent_rows, down_weight)
    gate_back = (back_hidden * up_proj * slope).astype(jnp.bfloat16)
    up_back = (back_hidden * active).astype(jnp.bfloat16)
    in_grad = lax.psum_scatter(
        (contract_cols(gate_back, gate_weight) + contract_cols(up_back, up_weight)).astype(
            jnp.bfloat16
        ),
        "dp",
        scatter_dimension=0,
        tiled=True,
    )
    gate_part = contract_rows(token_rows, gate_back)
    up_part = contract_rows(token_rows, up_back)
    down_part = contract_rows(hidden, cotangent_rows)
    gate_total, up_total, down_total = (
        lax.psum_scatter(
            gate_part.astype(jnp.bfloat16), "seq", scatter_dimension=0, tiled=True
        ).astype(jnp.float32),
        lax.psum_scatter(
            up_part.astype(jnp.bfloat16), "seq", scatter_dimension=0, tiled=True
        ).astype(jnp.float32),
        lax.psum_scatter(
            down_part.astype(jnp.bfloat16), "seq", scatter_dimension=1, tiled=True
        ).astype(jnp.float32),
    )
    return (
        output,
        in_grad,
        gate_total.astype(jnp.bfloat16),
        up_total.astype(jnp.bfloat16),
        down_total.astype(jnp.bfloat16),
    )


def solution(mesh):
    placed = (
        P(("dp", "seq"), None),
        P(("dp", "seq")),
        P(None, "dp"),
        P(None, "dp"),
        P("dp", None),
        P(("dp", "seq"), None),
    )
    return jax.shard_map(
        on_device,
        mesh=mesh,
        in_specs=placed,
        out_specs=(
            P(("dp", "seq"), None),
            P(("dp", "seq"), None),
            P("seq", "dp"),
            P("seq", "dp"),
            P("dp", "seq"),
        ),
        check_vma=False,
    )
```

profile of v0, /device:TPU:1, one launch (start us, length us, event | category | flops | bytes accessed | tf_op | source)
XLA Modules:
  0.0 548.4 jit_solution(6093787396927904217)
XLA Ops:
  7.2 0.0 all-gather.3.cloned.1.call-start
  7.2 0.7 fusion.5
  7.9 0.1 copy.12
  8.0 0.1 reduce-window.8
  8.1 0.1 add_reduce_fusion
  8.2 0.9 convolution_convert_fusion.4
  9.1 0.0 all-gather.5.cloned.1.call-start
  9.1 0.7 all-gather.5.cloned.1.call-update
  9.8 0.0 reduce-scatter.6.cloned.1.call-start
  9.9 55.7 %all-gather.3.cloned.1.call-done = bf16[384,4096]{1,0:T(8,128)(2,1)} async-done(((bf16[24,4096]{1,0:T(8,128)(2,1)}), bf16[384,4096]{1,0:T(8,128)(2,1)}) %all-gather.3.cloned.1.call-update) | async-done | bytes 3145744 | tf_op jit(solution)/shard_map/all_gather | solution.py:31
  65.6 8.6 %fusion.8 = f32[384,896]{1,0:T(8,128)S(1)} fusion(bf16[384,4096]{1,0:T(8,128)(2,1)} %all-gather.3.cloned.1.call-done, bf16[4096,896]{1,0:T(8,128)(2,1)} %param.9), kind=kOutput, calls=%fused_computation.20 | convolution fusion | flops 2818572288 | bytes 11862016 | tf_op jit(solution)/shard_map/dot_general | solution.py:33
  74.3 5.8 %fusion.7 = f32[384,896]{1,0:T(8,128)S(1)} fusion(bf16[384,4096]{1,0:T(8,128)(2,1)S(1)} %copy-done.2, bf16[4096,896]{1,0:T(8,128)(2,1)} %param.8), kind=kOutput, calls=%fused_computation.19 | convolution fusion | flops 2818572288 | bytes 11862016 | tf_op jit(solution)/shard_map/dot_general | solution.py:32
  80.0 37.6 %all-gather.5.cloned.1.call-done = bf16[384,4096]{1,0:T(8,128)(2,1)} async-done(((bf16[24,4096]{1,0:T(8,128)(2,1)}), bf16[384,4096]{1,0:T(8,128)(2,1)}) %all-gather.5.cloned.1.call-update) | async-done | bytes 3145744 | tf_op jit(solution)/shard_map/all_gather | solution.py:42
  117.7 8.9 %multiply_convert_fusion = (bf16[384,896]{1,0:T(8,128)(2,1)}, bf16[384,896]{1,0:T(8,128)(2,1)}, bf16[384,896]{1,0:T(8,128)(2,1)S(1)}) fusion(f32[384,896]{1,0:T(8,128)S(1)} %fusion.7, f32[384,896]{1,0:T(8,128)S(1)} %fusion.8, bf16[384,4096]{1,0:T(8,128)(2,1)} %all-gather.5.cloned.1.call-done, bf16[896,4096]{1,0:T(8,128)(2,1)} %param.10), kind=kOutput, calls=%fused_computation.6 | convolution fusion | flops 2823733248 | bytes 15302656 | tf_op jit(solution)/shard_map/dot_general | solution.py:19
  126.5 0.8 copy-done.6
  127.4 8.0 %convolution_convert_fusion.3 = bf16[384,4096]{1,0:T(8,128)(2,1)} fusion(bf16[384,896]{1,0:T(8,128)(2,1)S(1)} %get-tuple-element.7, bf16[896,4096]{1,0:T(8,128)(2,1)} %param.10), kind=kOutput, calls=%fused_computation.4 | convolution fusion | flops 2820145152 | bytes 11173888 | tf_op jit(solution)/shard_map/dot_general | solution.py:37
  135.5 0.0 reduce-scatter.8.cloned.1.call-start
  135.5 6.0 %fusion.9 = f32[384,4096]{1,0:T(8,128)S(1)} fusion(bf16[384,896]{1,0:T(8,128)(2,1)} %get-tuple-element.6, bf16[4096,896]{1,0:T(8,128)(2,1)} %param.8), kind=kOutput, calls=%fused_computation.21 | convolution fusion | flops 2818572288 | bytes 14319616 | tf_op jit(solution)/shard_map/dot_general | solution.py:19
  141.6 5.0 add_convert_fusion
  146.6 0.2 reduce-scatter.14.cloned.1.call-start
  146.8 1.8 copy-done.4
  148.6 7.1 %convolution_convert_fusion = bf16[896,4096]{1,0:T(8,128)(2,1)} fusion(bf16[384,896]{1,0:T(8,128)(2,1)} %copy-done.6, bf16[384,4096]{1,0:T(8,128)(2,1)S(1)} %copy-done.4), kind=kOutput, calls=%fused_computation | convolution fusion | flops 2822242304 | bytes 11173888 | tf_op jit(solution)/shard_map/dot_general | solution.py:13
  155.8 0.0 reduce-scatter.12.cloned.1.call-start
  155.8 1.9 copy-done.3
  157.7 7.5 %convolution_convert_fusion.1 = bf16[4096,896]{1,0:T(8,128)(2,1)} fusion(bf16[384,4096]{1,0:T(8,128)(2,1)S(1)} %copy-done.3, bf16[384,896]{1,0:T(8,128)(2,1)} %get-tuple-element.5), kind=kOutput, calls=%fused_computation.1 | convolution fusion | flops 2822242304 | bytes 11173888 | tf_op jit(solution)/shard_map/dot_general | solution.py:13
  165.2 0.0 reduce-scatter.10.cloned.1.call-start
  165.2 7.5 %convolution_convert_fusion.2 = bf16[4096,896]{1,0:T(8,128)(2,1)} fusion(bf16[384,4096]{1,0:T(8,128)(2,1)S(1)} %copy-done.3, bf16[384,896]{1,0:T(8,128)(2,1)} %get-tuple-element.6), kind=kOutput, calls=%fused_computation.2 | convolution fusion | flops 2822242304 | bytes 11173888 | tf_op jit(solution)/shard_map/dot_general | solution.py:13
  172.8 35.4 %reduce-scatter.6.cloned.1.call-done = bf16[24,4096]{1,0:T(8,128)(2,1)} async-done(((bf16[384,4096]{1,0:T(8,128)(2,1)}), bf16[24,4096]{1,0:T(8,128)(2,1)}) %reduce-scatter.6.cloned.1.call-update) | async-done | bytes 196624 | tf_op jit(solution)/shard_map/reduce_scatter | solution.py:36
  208.2 78.8 %reduce-scatter.8.cloned.1.call-done = bf16[24,4096]{1,0:T(8,128)(2,1)} async-done(((bf16[384,4096]{1,0:T(8,128)(2,1)}), bf16[24,4096]{1,0:T(8,128)(2,1)}) %reduce-scatter.8.cloned.1.call-update) | async-done | bytes 196624 | tf_op jit(solution)/shard_map/reduce_scatter | solution.py:46
  286.9 85.6 %reduce-scatter.14.cloned.1.call-done = bf16[896,512]{1,0:T(8,128)(2,1)} async-done(((bf16[896,4096]{1,0:T(8,128)(2,1)}), bf16[896,512]{1,0:T(8,128)(2,1)}) %reduce-scatter.14.cloned.1.call-update) | async-done | bytes 917520 | tf_op jit(solution)/shard_map/reduce_scatter | solution.py:64
  372.5 84.5 %reduce-scatter.12.cloned.1.call-done = bf16[512,896]{1,0:T(8,128)(2,1)} async-done(((bf16[4096,896]{1,0:T(8,128)(2,1)}), bf16[512,896]{1,0:T(8,128)(2,1)}) %reduce-scatter.12.cloned.1.call-update) | async-done | bytes 917520 | tf_op jit(solution)/shard_map/reduce_scatter | solution.py:61
  457.0 84.6 %reduce-scatter.10.cloned.1.call-done = bf16[512,896]{1,0:T(8,128)(2,1)} async-done(((bf16[4096,896]{1,0:T(8,128)(2,1)}), bf16[512,896]{1,0:T(8,128)(2,1)}) %reduce-scatter.10.cloned.1.call-update) | async-done | bytes 917520 | tf_op jit(solution)/shard_map/reduce_scatter | solution.py:58
  (22 shorter events, 0.1 us)
Async XLA Ops:
  7.2 1.0 copy-start
  7.2 58.4 %all-gather.3.cloned.1.call-start = ((), (), s32[]{:S(2)}) async-start(), calls=%async_computation.5 | async-start | bytes 3342336 | tf_op jit(solution)/shard_map/all_gather | solution.py:31
  9.1 108.6 %all-gather.5.cloned.1.call-start = ((), (), s32[]{:S(2)}) async-start(), calls=%async_computation.7 | async-start | bytes 3342336 | tf_op jit(solution)/shard_map/all_gather | solution.py:42
  9.8 198.3 %reduce-scatter.6.cloned.1.call-start = ((), (), s32[]{:S(2)}) async-start(), calls=%async_computation.6 | async-start | bytes 3342336 | tf_op jit(solution)/shard_map/reduce_scatter | solution.py:36
  65.6 8.6 %copy-start.2 = (bf16[384,4096]{1,0:T(8,128)(2,1)S(1)}, bf16[384,4096]{1,0:T(8,128)(2,1)}, u32[]{:S(2)}) copy-start(bf16[384,4096]{1,0:T(8,128)(2,1)} %all-gather.3.cloned.1.call-done) | copy-start | bytes 9437188
  126.5 0.8 copy-start.6
  135.4 6.1 %slice-start = ((s8[7340032]{0:T(1024)(128)(4,1)}), s8[3145728]{0:T(1024)(128)(4,1)S(1)}, s32[]{:S(2)}) async-start(s8[7340032]{0:T(1024)(128)(4,1)} %bitcast.21), calls=%async_computation.12 | async-start | bytes 6291456
  135.5 151.5 %reduce-scatter.8.cloned.1.call-start = ((), (), s32[]{:S(2)}) async-start(), calls=%async_computation.8 | async-start | bytes 3342336 | tf_op jit(solution)/shard_map/reduce_scatter | solution.py:46
  135.5 6.1 %slice-start.1 = ((s8[7340032]{0:T(1024)(128)(4,1)}), s8[4194304]{0:T(1024)(128)(4,1)S(1)}, s32[]{:S(2)}) async-start(s8[7340032]{0:T(1024)(128)(4,1)} %bitcast.21), calls=%async_computation.13 | async-start | bytes 8388608
  135.5 6.1 %copy-start.5 = (bf16[384,896]{1,0:T(8,128)(2,1)S(1)}, bf16[384,896]{1,0:T(8,128)(2,1)}, u32[]{:S(2)}) copy-start(bf16[384,896]{1,0:T(8,128)(2,1)} %get-tuple-element.5) | copy-start | bytes 2064388
  146.6 2.0 copy-start.4
  146.6 225.9 %reduce-scatter.14.cloned.1.call-start = ((), (), s32[]{:S(2)}) async-start(), calls=%async_computation.11 | async-start | bytes 8257536 | tf_op jit(solution)/shard_map/reduce_scatter | solution.py:64
  155.7 1.9 copy-start.3
  155.8 301.2 %reduce-scatter.12.cloned.1.call-start = ((), (), s32[]{:S(2)}) async-start(), calls=%async_computation.10 | async-start | bytes 8257536 | tf_op jit(solution)/shard_map/reduce_scatter | solution.py:61
  165.2 376.4 %reduce-scatter.10.cloned.1.call-start = ((), (), s32[]{:S(2)}) async-start(), calls=%async_computation.9 | async-start | bytes 8257536 | tf_op jit(solution)/shard_map/reduce_scatter | solution.py:58
  172.8 368.8 %copy-start.1 = (bf16[32,4096]{1,0:T(8,128)(2,1)S(1)}, bf16[32,4096]{1,0:T(8,128)(2,1)}, u32[]{:S(2)}) copy-start(bf16[32,4096]{1,0:T(8,128)(2,1)} %param.6) | copy-start | bytes 786436
Sparse Core Ops, SparseCore 0:
  11.0 54.5 all-gather.2
  68.1 49.5 all-gather.4
  135.6 72.5 reduce-scatter.5
  212.7 74.2 reduce-scatter.7
  289.8 82.6 reduce-scatter.13
  375.4 81.5 reduce-scatter.11
  460.0 81.5 reduce-scatter.9
where the time goes:
time: 549 us; the launch traced here: 548 us
  waiting for transfers between devices  463 us (84%)
  matrix products  65.3 us (12%)
  between operations  14.2 us (3%)
    reduce_scatter x1, waiting for transfers between devices, on_device(): lax.psum_scatter(down_part.astype(jnp.bfloat16), 'seq', scatter_dimension...  85.6 us
    reduce_scatter x1, waiting for transfers between devices, on_device(): lax.psum_scatter(gate_part.astype(jnp.bfloat16), 'seq', scatter_dimension...  84.6 us
    reduce_scatter x1, waiting for transfers between devices, on_device(): lax.psum_scatter(up_part.astype(jnp.bfloat16), 'seq', scatter_dimension=0...  84.5 us
    reduce_scatter x1, waiting for transfers between devices, on_device(): lax.psum_scatter((contract_cols(gate_back, gate_weight) + contract_cols(u...  78.8 us
    all_gather x1, waiting for transfers between devices, on_device(): token_rows = lax.all_gather(picked, 'dp', axis=0, tiled=True)  55.7 us
    all_gather x1, waiting for transfers between devices, on_device(): cotangent_rows = lax.all_gather(out_grad, 'dp', axis=0, tiled=True)  37.6 us
    reduce_scatter x1, waiting for transfers between devices, on_device(): lax.psum_scatter(jnp.dot(hidden, down_weight, preferred_element_type=jnp....  35.4 us
    dot_general x3, matrix products, contract_rows(): lax.dot_general(left_matrix, right_matrix, (((0,), (0,)), ((), ())), pref...  22.2 us
  transfers between devices with their start and end apart: 7, of which 7 were waited for; matrix products, arithmetic and copies ran while one was open for 9% of the time, Pallas kernels for 0%

commit v1 on v0

--- a/solution.py
+++ b/solution.py
@@ -39,7 +39,9 @@
         scatter_dimension=0,
         tiled=True,
     )
-    cotangent_rows = lax.all_gather(out_grad, "dp", axis=0, tiled=True)
+    cotangent_rows = jnp.concatenate(
+        lax.all_to_all(jnp.stack([out_grad] * lax.axis_size("dp")), "dp", 0, 0), axis=0
+    )
     back_hidden = contract_cols(cotangent_rows, down_weight)
     gate_back = (back_hidden * up_proj * slope).astype(jnp.bfloat16)
     up_back = (back_hidden * active).astype(jnp.bfloat16)

time: 549 us -> 532 us (0.969)
  waiting for transfers between devices: 463 us -> 429 us
  starting transfers between devices: 0.46 us -> 9.88 us
  matrix products: 65.3 us -> 71.9 us
    all_gather x1 -> x0, waiting for transfers between devices: 37.6 us -> none  [on_device(): cotangent_rows = lax.all_gather(out_grad, 'dp', axis=0, tiled=True)]
    all_to_all x0 -> x1, starting transfers between devices: none -> 9.46 us  [on_device(): lax.all_to_all(jnp.stack([out_grad] * lax.axis_size('dp')), 'dp', 0, 0)]
    all_gather x1, waiting for transfers between devices: 55.7 us -> 63.5 us  [on_device(): token_rows = lax.all_gather(picked, 'dp', axis=0, tiled=True)]
  transfers between devices with their start and end apart: 7 -> 7, of which waited for: 7 -> 6; matrix products, arithmetic and copies ran while one was open for 9% -> 11% of each run, Pallas kernels for 0% -> 0%
where the time goes in v1:
time: 532 us
  waiting for transfers between devices  429 us (81%)
  matrix products  71.9 us (14%)
  between operations  14.2 us (3%)
  starting transfers between devices  9.88 us (2%)
  local copies, waits for them, and re-layouts  5.72 us (1%)
    reduce_scatter x1, waiting for transfers between devices, on_device(): lax.psum_scatter(down_part.astype(jnp.bfloat16), 'seq', scatter_dimension...  85.6 us
    reduce_scatter x1, waiting for transfers between devices, on_device(): lax.psum_scatter(gate_part.astype(jnp.bfloat16), 'seq', scatter_dimension...  84.4 us
    reduce_scatter x1, waiting for transfers between devices, on_device(): lax.psum_scatter(up_part.astype(jnp.bfloat16), 'seq', scatter_dimension=0...  84.4 us
    reduce_scatter x1, waiting for transfers between devices, on_device(): lax.psum_scatter((contract_cols(gate_back, gate_weight) + contract_cols(u...  78.9 us
    all_gather x1, waiting for transfers between devices, on_device(): token_rows = lax.all_gather(picked, 'dp', axis=0, tiled=True)  63.5 us
    reduce_scatter x1, waiting for transfers between devices, on_device(): lax.psum_scatter(jnp.dot(hidden, down_weight, preferred_element_type=jnp....  32.5 us
    dot_general x3, matrix products, contract_cols(): lax.dot_general(left_matrix, right_matrix, (((1,), (1,)), ((), ())), pref...  25.4 us
    dot_general x3, matrix products, contract_rows(): lax.dot_general(left_matrix, right_matrix, (((0,), (0,)), ((), ())), pref...  22.2 us
  transfers between devices with their start and end apart: 7, of which 6 were waited for; matrix products, arithmetic and copies ran while one was open for 11% of the time, Pallas kernels for 0%

profile of v1, /device:TPU:1, one launch (start us, length us, event | category | flops | bytes accessed | tf_op | source)
XLA Modules:
  0.0 531.9 jit_solution(2619268925249998542)
XLA Ops:
  7.2 0.0 all-gather.2.cloned.1.call-start
  7.2 0.7 fusion.5
  7.9 0.1 copy.12
  8.0 0.1 reduce-window.8
  8.1 0.1 add_reduce_fusion
  8.2 0.9 convolution_convert_fusion.4
  9.1 2.9 stack.2
  12.0 9.5 %all-to-all-start = ((bf16[16,24,4096]{2,1,0:T(8,128)(2,1)}), bf16[16,24,4096]{2,1,0:T(8,128)(2,1)S(1)}, u32[]{:S(2)}, u32[]{:S(2)}) async-start(bf16[16,24,4096]{2,1,0:T(8,128)(2,1)} %stack.2), calls=%async_computation.1 | async-start | bytes 6291456 | tf_op jit(solution)/shard_map/all_to_all | solution.py:43
  21.5 0.0 reduce-scatter.6.cloned.1.call-start
  21.5 63.5 %all-gather.2.cloned.1.call-done = bf16[384,4096]{1,0:T(8,128)(2,1)} async-done(((bf16[24,4096]{1,0:T(8,128)(2,1)}), bf16[384,4096]{1,0:T(8,128)(2,1)}) %all-gather.2.cloned.1.call-update) | async-done | bytes 3145744 | tf_op jit(solution)/shard_map/all_gather | solution.py:31
  85.0 8.7 %fusion.8 = f32[384,896]{1,0:T(8,128)} fusion(bf16[384,4096]{1,0:T(8,128)(2,1)} %all-gather.2.cloned.1.call-done, bf16[4096,896]{1,0:T(8,128)(2,1)} %param.9), kind=kOutput, calls=%fused_computation.20 | convolution fusion | flops 2818572288 | bytes 11862016 | tf_op jit(solution)/shard_map/dot_general | solution.py:33
  93.7 6.8 %fusion.7 = f32[384,896]{1,0:T(8,128)} fusion(bf16[384,4096]{1,0:T(8,128)(2,1)S(1)} %copy-done.2, bf16[4096,896]{1,0:T(8,128)(2,1)} %param.8), kind=kOutput, calls=%fused_computation.19 | convolution fusion | flops 2818572288 | bytes 11862016 | tf_op jit(solution)/shard_map/dot_general | solution.py:32
  100.5 9.6 %multiply_convert_fusion = (bf16[384,896]{1,0:T(8,128)(2,1)}, bf16[384,896]{1,0:T(8,128)(2,1)}, bf16[384,896]{1,0:T(8,128)(2,1)S(1)}) fusion(f32[384,896]{1,0:T(8,128)} %fusion.7, f32[384,896]{1,0:T(8,128)} %fusion.8, bf16[384,4096]{1,0:T(8,128)(2,1)S(1)} %bitcast.22, bf16[896,4096]{1,0:T(8,128)(2,1)} %param.10), kind=kOutput, calls=%fused_computation.6 | convolution fusion | flops 2823733248 | bytes 15302656 | tf_op jit(solution)/shard_map/dot_general | solution.py:19
  110.1 0.8 copy-done.5
  111.0 8.0 %convolution_convert_fusion.3 = bf16[384,4096]{1,0:T(8,128)(2,1)} fusion(bf16[384,896]{1,0:T(8,128)(2,1)S(1)} %get-tuple-element.7, bf16[896,4096]{1,0:T(8,128)(2,1)} %param.10), kind=kOutput, calls=%fused_computation.4 | convolution fusion | flops 2820145152 | bytes 11173888 | tf_op jit(solution)/shard_map/dot_general | solution.py:37
  119.0 0.0 reduce-scatter.6.cloned.1.call-update
  119.0 0.0 reduce-scatter.8.cloned.1.call-start
  119.1 6.0 %fusion.9 = f32[384,4096]{1,0:T(8,128)S(1)} fusion(bf16[384,896]{1,0:T(8,128)(2,1)} %get-tuple-element.6, bf16[4096,896]{1,0:T(8,128)(2,1)} %param.8), kind=kOutput, calls=%fused_computation.21 | convolution fusion | flops 2818572288 | bytes 14319616 | tf_op jit(solution)/shard_map/dot_general | solution.py:19
  125.1 9.8 %add_convert_fusion = bf16[384,4096]{1,0:T(8,128)(2,1)} fusion(f32[384,4096]{1,0:T(8,128)S(1)} %fusion.9, bf16[384,896]{1,0:T(8,128)(2,1)S(1)} %copy-done.4, bf16[4096,896]{1,0:T(8,128)(2,1)} %param.9), kind=kOutput, calls=%fused_computation.3 | convolution fusion | flops 2821718016 | bytes 17465344 | tf_op jit(solution)/shard_map/dot_general | solution.py:19
  134.9 0.2 reduce-scatter.14.cloned.1.call-start
  135.1 7.2 %convolution_convert_fusion = bf16[896,4096]{1,0:T(8,128)(2,1)} fusion(bf16[384,896]{1,0:T(8,128)(2,1)} %copy-done.5, bf16[384,4096]{1,0:T(8,128)(2,1)S(1)} %bitcast.23), kind=kOutput, calls=%fused_computation | convolution fusion | flops 2822242304 | bytes 11173888 | tf_op jit(solution)/shard_map/dot_general | solution.py:13
  142.2 0.0 reduce-scatter.14.cloned.1.call-update
  142.3 0.0 reduce-scatter.12.cloned.1.call-start
  142.3 1.8 copy-done.3
  144.1 7.5 %convolution_convert_fusion.1 = bf16[4096,896]{1,0:T(8,128)(2,1)} fusion(bf16[384,4096]{1,0:T(8,128)(2,1)S(1)} %copy-done.3, bf16[384,896]{1,0:T(8,128)(2,1)} %get-tuple-element.5), kind=kOutput, calls=%fused_computation.1 | convolution fusion | flops 2822242304 | bytes 11173888 | tf_op jit(solution)/shard_map/dot_general | solution.py:13
  151.6 0.0 reduce-scatter.10.cloned.1.call-start
  151.7 7.6 %convolution_convert_fusion.2 = bf16[4096,896]{1,0:T(8,128)(2,1)} fusion(bf16[384,4096]{1,0:T(8,128)(2,1)S(1)} %copy-done.3, bf16[384,896]{1,0:T(8,128)(2,1)} %get-tuple-element.6), kind=kOutput, calls=%fused_computation.2 | convolution fusion | flops 2822242304 | bytes 11173888 | tf_op jit(solution)/shard_map/dot_general | solution.py:13
  159.3 32.5 %reduce-scatter.6.cloned.1.call-done = bf16[24,4096]{1,0:T(8,128)(2,1)} async-done(((bf16[384,4096]{1,0:T(8,128)(2,1)}), bf16[24,4096]{1,0:T(8,128)(2,1)}) %reduce-scatter.6.cloned.1.call-update) | async-done | bytes 196624 | tf_op jit(solution)/shard_map/reduce_scatter | solution.py:36
  191.7 78.9 %reduce-scatter.8.cloned.1.call-done = bf16[24,4096]{1,0:T(8,128)(2,1)} async-done(((bf16[384,4096]{1,0:T(8,128)(2,1)}), bf16[24,4096]{1,0:T(8,128)(2,1)}) %reduce-scatter.8.cloned.1.call-update) | async-done | bytes 196624 | tf_op jit(solution)/shard_map/reduce_scatter | solution.py:48
  270.6 85.6 %reduce-scatter.14.cloned.1.call-done = bf16[896,512]{1,0:T(8,128)(2,1)} async-done(((bf16[896,4096]{1,0:T(8,128)(2,1)}), bf16[896,512]{1,0:T(8,128)(2,1)}) %reduce-scatter.14.cloned.1.call-update) | async-done | bytes 917520 | tf_op jit(solution)/shard_map/reduce_scatter | solution.py:66
  356.2 84.4 %reduce-scatter.12.cloned.1.call-done = bf16[512,896]{1,0:T(8,128)(2,1)} async-done(((bf16[4096,896]{1,0:T(8,128)(2,1)}), bf16[512,896]{1,0:T(8,128)(2,1)}) %reduce-scatter.12.cloned.1.call-update) | async-done | bytes 917520 | tf_op jit(solution)/shard_map/reduce_scatter | solution.py:63
  440.7 84.4 %reduce-scatter.10.cloned.1.call-done = bf16[512,896]{1,0:T(8,128)(2,1)} async-done(((bf16[4096,896]{1,0:T(8,128)(2,1)}), bf16[512,896]{1,0:T(8,128)(2,1)}) %reduce-scatter.10.cloned.1.call-update) | async-done | bytes 917520 | tf_op jit(solution)/shard_map/reduce_scatter | solution.py:60
  (15 shorter events, 0.1 us)
Async XLA Ops:
  7.2 1.0 copy-start
  7.2 77.8 %all-gather.2.cloned.1.call-start = ((), (), s32[]{:S(2)}) async-start(), calls=%async_computation.6 | async-start | bytes 3342336 | tf_op jit(solution)/shard_map/all_gather | solution.py:31
  12.0 88.5 %all-to-all-start = ((bf16[16,24,4096]{2,1,0:T(8,128)(2,1)}), bf16[16,24,4096]{2,1,0:T(8,128)(2,1)S(1)}, u32[]{:S(2)}, u32[]{:S(2)}) async-start(bf16[16,24,4096]{2,1,0:T(8,128)(2,1)} %stack.2), calls=%async_computation.1 | async-start | bytes 6291456 | tf_op jit(solution)/shard_map/all_to_all | solution.py:43
  21.5 170.2 %reduce-scatter.6.cloned.1.call-start = ((), (), s32[]{:S(2)}) async-start(), calls=%async_computation.7 | async-start | bytes 3342336 | tf_op jit(solution)/shard_map/reduce_scatter | solution.py:36
  85.0 8.7 %copy-start.2 = (bf16[384,4096]{1,0:T(8,128)(2,1)S(1)}, bf16[384,4096]{1,0:T(8,128)(2,1)}, u32[]{:S(2)}) copy-start(bf16[384,4096]{1,0:T(8,128)(2,1)} %all-gather.2.cloned.1.call-done) | copy-start | bytes 9437188
  110.1 0.8 copy-start.5
  119.0 151.6 %reduce-scatter.8.cloned.1.call-start = ((), (), s32[]{:S(2)}) async-start(), calls=%async_computation.8 | async-start | bytes 3342336 | tf_op jit(solution)/shard_map/reduce_scatter | solution.py:48
  119.1 6.0 %copy-start.4 = (bf16[384,896]{1,0:T(8,128)(2,1)S(1)}, bf16[384,896]{1,0:T(8,128)(2,1)}, u32[]{:S(2)}) copy-start(bf16[384,896]{1,0:T(8,128)(2,1)} %get-tuple-element.5) | copy-start | bytes 2064388
  134.9 221.4 %reduce-scatter.14.cloned.1.call-start = ((), (), s32[]{:S(2)}) async-start(), calls=%async_computation.11 | async-start | bytes 8257536 | tf_op jit(solution)/shard_map/reduce_scatter | solution.py:66
  142.2 1.9 copy-start.3
  142.3 298.4 %reduce-scatter.12.cloned.1.call-start = ((), (), s32[]{:S(2)}) async-start(), calls=%async_computation.10 | async-start | bytes 8257536 | tf_op jit(solution)/shard_map/reduce_scatter | solution.py:63
  151.6 373.5 %reduce-scatter.10.cloned.1.call-start = ((), (), s32[]{:S(2)}) async-start(), calls=%async_computation.9 | async-start | bytes 8257536 | tf_op jit(solution)/shard_map/reduce_scatter | solution.py:60
  159.2 365.9 %copy-start.1 = (bf16[32,4096]{1,0:T(8,128)(2,1)S(1)}, bf16[32,4096]{1,0:T(8,128)(2,1)}, u32[]{:S(2)}) copy-start(bf16[32,4096]{1,0:T(8,128)(2,1)} %param.6) | copy-start | bytes 786436
Sparse Core Ops, SparseCore 0:
  11.0 73.9 all-gather.1
  119.1 72.5 reduce-scatter.5
  196.4 74.2 reduce-scatter.7
  273.5 82.7 reduce-scatter.13
  359.1 81.5 reduce-scatter.11
  443.5 81.5 reduce-scatter.9
